TPU v7x, 256 devices: a whole 4x4x8 slice. The times are simulated.
256 devices in a mesh: seq: 64 (over x, z, core), head: 4 (over y).
Axes of the slice: x: 4, y: 4, z: 8, core: 2. Of those that a mesh axis runs over, the one named last changes fastest.
Arguments:
- frames: bfloat16 [16384, 1024], P('seq'), may hold values from -6 to 6
- norm_gain: float32 [1024], replicated, may hold values from 0.5 to 1.5
- w_qkv: bfloat16 [3, 1024, 1024], P(None, None, 'head'), may hold values from -2 to 2
- w_out: bfloat16 [1024, 1024], P('head'), may hold values from -0.1875 to 0.1875
- w_proj: bfloat16 [1024, 512], replicated, may hold values from -0.1875 to 0.1875
- text_table: bfloat16 [32768, 512], P(('seq', 'head')), may hold values from -6 to 6
- token_ids: int32 [512, 16], replicated, may hold values from 0 to 32767
- span_bounds: int32 [512, 2], P(('seq', 'head')), may hold values from 0 to 16384, as said below
- contrast_divisor: float32 [1], replicated, may hold values from 10 to 30
Outputs:
- interval_embedding_derivative: float32 [512, 512], P(('seq', 'head'))
- loss_terms: float32 [512], P(('seq', 'head'))
Inputs may be any that keep to these rules, and one draw needn't show every extreme that they name: `span_bounds`: both entries are multiples of 128 and the first is smaller than the second.
All inputs are finite; a program needn't handle non-finite values.
Results may differ from a plain program's by a relative error of at most 0.006.
Values may be sent and summed in bfloat16 or wider, within the bound.
A program may use at most 64 MiB of HBM per device.

v0:
```python
import jax
import jax.numpy as jnp
from jax import lax
from jax.sharding import PartitionSpec as P

HDIM = 64
E = 512
BLK = 128


def extended(cells, sides, width):
    for axis, dim in sides:
        count = lax.axis_size(axis)
        ends = count - 1
        head = lax.slice_in_dim(cells, 0, width, axis=dim)
        tail = lax.slice_in_dim(cells, cells.shape[dim] - width, cells.shape[dim], axis=dim)
        cells = jnp.concatenate(
            [
                lax.ppermute(tail, axis, [(i, (i + 1) % count) for i in range(ends)]),
                cells,
                lax.ppermute(head, axis, [((i + 1) % count, i) for i in range(ends)]),
            ],
            axis=dim,
        )
    return cells


def log_total(values, axis):
    return jnp.log(jnp.sum(jnp.exp(values), axis=axis))


def unit_rows(values):
    return (
        values * lax.rsqrt(jnp.mean(values * values, axis=-1, keepdims=True) + 1e-06) * E ** (-0.5)
    )


def token_counts(chosen, vocab_ids):

    def add_token(position, counts):
        column = lax.dynamic_index_in_dim(chosen, position, 1, keepdims=False)
        return counts + (column[:, None] == vocab_ids[None, :]).astype(jnp.float32)

    return lax.fori_loop(
        0, chosen.shape[1], add_token, jnp.zeros((chosen.shape[0], vocab_ids.shape[0]), jnp.float32)
    )


def local(
    frames, norm_gain, w_qkv, w_out, w_proj, text_table, token_ids, span_bounds, contrast_divisor
):
    frame_rows = frames.shape[0]
    head_cols = w_qkv.shape[2]
    local_heads = head_cols // HDIM
    seq_count = lax.axis_size("seq")
    total_frames = frame_rows * seq_count
    first_frame = lax.axis_index("seq") * frame_rows
    as32 = frames.astype(jnp.float32)
    normed = (
        as32 * lax.rsqrt(jnp.mean(as32 * as32, axis=-1, keepdims=True) + 1e-05) * norm_gain
    ).astype(jnp.bfloat16)
    queries = jnp.dot(normed, w_qkv[0], preferred_element_type=jnp.float32).astype(jnp.bfloat16)
    keys_now = jnp.dot(normed, w_qkv[1], preferred_element_type=jnp.float32).astype(jnp.bfloat16)
    values_now = jnp.dot(normed, w_qkv[2], preferred_element_type=jnp.float32).astype(jnp.bfloat16)
    pairs = jnp.concatenate([keys_now, values_now], axis=1)
    padded = extended(pairs, (("seq", 0),), frame_rows)
    query_block = min(512, frame_rows)
    span_width = 2 * frame_rows + query_block

    def attend(block):
        begin = block * query_block
        query_part = queries.reshape(query_block, local_heads, HDIM)
        key_part = padded[:, :head_cols].reshape(span_width, local_heads, HDIM)
        value_part = padded[:, head_cols:].reshape(span_width, local_heads, HDIM)
        scores = jnp.einsum(
            "qhd,khd->hqk", query_part, key_part, preferred_element_type=jnp.float32
        ) * HDIM ** (-0.5)
        query_pos = first_frame + begin + jnp.arange(query_block, dtype=jnp.int32)
        key_pos = first_frame + begin - frame_rows + jnp.arange(span_width, dtype=jnp.int32)
        allowed = (
            (jnp.abs(query_pos[:, None] - key_pos[None, :]) <= frame_rows)
            & (key_pos >= 0)[None, :]
            & (key_pos < total_frames)[None, :]
        )
        scores = jnp.where(allowed[None], scores, -1e30)
        top = jnp.max(scores, axis=2, keepdims=True)
        probs = jnp.exp(scores - top)
        denom = jnp.sum(probs, axis=2)
        mixed = jnp.einsum(
            "hqk,khd->qhd",
            probs.astype(jnp.bfloat16),
            value_part,
            preferred_element_type=jnp.float32,
        )
        return (mixed / denom.T[:, :, None]).astype(jnp.bfloat16).reshape(query_block, head_cols)

    attended = lax.map(attend, jnp.arange(frame_rows // query_block, dtype=jnp.int32)).reshape(
        frame_rows, head_cols
    )
    block_count = frame_rows // BLK
    out_sums = attended.astype(jnp.float32).reshape(block_count, BLK, head_cols).sum(axis=1)
    head_slot = lax.axis_index("head")
    own_features = lax.dynamic_slice_in_dim(as32, head_slot * head_cols, head_cols, 1)
    feature_sums = own_features.reshape(block_count, BLK, head_cols).sum(axis=1)
    proj_rows = lax.dynamic_slice_in_dim(w_proj, head_slot * head_cols, head_cols, 0)
    through_out = jnp.dot(out_sums, w_out.astype(jnp.float32), precision=lax.Precision.HIGHEST)
    partial_value = jnp.dot(
        through_out, w_proj.astype(jnp.float32), precision=lax.Precision.HIGHEST
    ) + jnp.dot(feature_sums, proj_rows.astype(jnp.float32), precision=lax.Precision.HIGHEST)
    everyone = lax.all_gather(partial_value, ("seq", "head"), axis=0, tiled=True)
    head_count = lax.axis_size("head")
    block_table = (
        everyone.reshape(seq_count, head_count, block_count, -1)
        .sum(axis=1)
        .reshape(seq_count * block_count, -1)
    )
    total_blocks = block_table.shape[0]
    block_ids = jnp.arange(total_blocks, dtype=jnp.int32)
    lower = span_bounds[:, 0] // BLK
    upper = span_bounds[:, 1] // BLK
    span_mask = (
        (block_ids[None, :] >= lower[:, None]) & (block_ids[None, :] < upper[:, None])
    ).astype(jnp.float32)
    pooled = jnp.dot(span_mask, block_table, precision=lax.Precision.HIGHEST)
    interval_embedding_rows = unit_rows(pooled).astype(jnp.bfloat16)
    own_caps = span_bounds.shape[0]
    all_caps = token_ids.shape[0]
    slot = lax.axis_index(("seq", "head"))
    first_caption = slot * own_caps
    vocab_rows = text_table.shape[0]
    vocab_ids = slot * vocab_rows + jnp.arange(vocab_rows, dtype=jnp.int32)
    counts = token_counts(token_ids, vocab_ids)
    raw = lax.psum_scatter(
        jnp.dot(counts.astype(jnp.bfloat16), text_table, preferred_element_type=jnp.float32),
        ("seq", "head"),
        scatter_dimension=0,
        tiled=True,
    )
    caption_own = unit_rows(raw).astype(jnp.bfloat16)
    spans_all, captions_all = (
        lax.all_gather(interval_embedding_rows, ("seq", "head"), axis=0, tiled=True),
        lax.all_gather(caption_own, ("seq", "head"), axis=0, tiled=True),
    )
    normalizer_divisor = contrast_divisor[0]
    row_logits = (
        jnp.einsum("je,ie->ji", caption_own, spans_all, preferred_element_type=jnp.float32)
        * normalizer_divisor
    )
    col_logits = (
        jnp.einsum(
            "je,ie->ji", captions_all, interval_embedding_rows, preferred_element_type=jnp.float32
        )
        * normalizer_divisor
    )
    row_total = log_total(row_logits, 1)
    col_total = log_total(col_logits, 0)
    own_square = lax.dynamic_slice_in_dim(row_logits, first_caption, own_caps, 1)
    loss_terms = 0.5 * (row_total + col_total) - jnp.diagonal(own_square)
    row_totals = lax.all_gather(row_total, ("seq", "head"), axis=0, tiled=True)
    marker = (
        jnp.arange(all_caps, dtype=jnp.int32)[:, None]
        == first_caption + jnp.arange(own_caps, dtype=jnp.int32)[None, :]
    ).astype(jnp.float32)
    derivative_multipliers = (
        0.5 * jnp.exp(col_logits - row_totals[:, None])
        + 0.5 * jnp.exp(col_logits - col_total[None, :])
        - marker
    ).astype(jnp.bfloat16)
    interval_embedding_derivative = (
        jnp.einsum(
            "ji,je->ie", derivative_multipliers, captions_all, preferred_element_type=jnp.float32
        )
        * normalizer_divisor
    )
    return (interval_embedding_derivative, loss_terms)


def solution(mesh):
    placed = (
        P("seq", None),
        P(),
        P(None, None, "head"),
        P("head", None),
        P(),
        P(("seq", "head"), None),
        P(),
        P(("seq", "head"), None),
        P(),
    )
    return jax.shard_map(
        local,
        mesh=mesh,
        in_specs=placed,
        out_specs=(P(("seq", "head"), None), P(("seq", "head"))),
        check_vma=False,
    )
```

profile of v0, /device:TPU:1, one launch (start us, length us, event | category | flops | bytes accessed | tf_op | source)
XLA Modules:
  0.0 622.0 jit_solution(1436011307544993010)
XLA Ops:
  7.2 1.3 multiply_reduce_fusion
  8.5 1.7 convolution_convert_fusion.1
  10.3 1.7 convolution_convert_fusion.2
  12.0 5.1 collective-permute-start
  17.0 2.2 collective-permute-start.1
  19.2 14.5 %while.18 = (s32[]{:T(128)}, f32[512,128]{1,0:T(8,128)S(1)}, s32[512,16]{0,1:T(8,128)}, s32[]{:T(128)}, s32[]{:T(128)}, /*index=5*/s32[]{:T(128)}) while((s32[]{:T(128)}, f32[512,128]{1,0:T(8,128)S(1)}, s32[512,16]{0,1:T(8,128)}, s32[]{:T(128)}, s32[]{:T(128)}, /*index=5*/s32[]{:T(128)}) %tuple.47), condition=%wide.region_1.2_spmd.clone, body=%wide.region_0.0_spmd.clone.sunk | while | flops 262275 | bytes 531543 | solution.py:44
  19.2 0.7 constant_dynamic-slice_fusion.4
  20.2 0.7 constant_dynamic-slice_fusion.4
  21.1 0.7 constant_dynamic-slice_fusion.4
  22.0 0.7 constant_dynamic-slice_fusion.4
  22.9 0.7 constant_dynamic-slice_fusion.4
  23.8 0.7 constant_dynamic-slice_fusion.4
  24.7 0.7 constant_dynamic-slice_fusion.4
  25.6 0.7 constant_dynamic-slice_fusion.4
  26.5 0.7 constant_dynamic-slice_fusion.4
  27.4 0.7 constant_dynamic-slice_fusion.4
  33.7 1.3 fusion.30
  35.7 1.5 convolution_convert_fusion
  37.2 1.1 pad_maximum_fusion
  38.4 0.8 fusion.2
  39.2 0.9 fusion.3
  40.1 1.0 fusion.18
  42.5 0.8 fusion.11
  44.4 251.9 %all-reduce.4.cloned.1.call-done = f32[512,512]{1,0:T(8,128)} async-done(((f32[512,512]{1,0:T(8,128)}), f32[512,512]{1,0:T(8,128)}) %all-reduce.4.cloned.1.call-update) | async-done | bytes 1048592
  296.3 0.8 multiply_reduce_fusion.2
  297.1 0.8 fusion.74
  297.9 118.1 %all-gather = bf16[256,2,512]{2,1,0:T(2,128)(2,1)S(1)} all-gather(bf16[1,2,512]{2,1,0:T(2,128)(2,1)S(1)} %fusion.74), channel_id=1, replica_groups=mesh['seq'=64,'head'=4] {'seq','head'}, dimensions={0}, use_global_device_ids=true | all-gather | bytes 526336 | tf_op jit(solution)/shard_map/all_gather | solution.py:142
  416.3 1.8 bitcast_reduce_fusion
  418.7 116.9 %all-gather.2 = bf16[256,2,512]{2,1,0:T(2,128)(2,1)S(1)} all-gather(bf16[1,2,512]{2,1,0:T(2,128)(2,1)S(1)} %fusion.73), channel_id=1, replica_groups=mesh['seq'=64,'head'=4] {'seq','head'}, dimensions={0}, use_global_device_ids=true | all-gather | bytes 526336 | tf_op jit(solution)/shard_map/all_gather | solution.py:141
  535.8 1.1 exponential_reduce_fusion.1
  538.5 75.9 %all-reduce = f32[512]{0:T(512)S(1)} all-reduce(f32[512]{0:T(512)S(1)} %get-tuple-element.129), channel_id=1, replica_groups=mesh['seq'=64,'head'=4] {'seq','head'}, use_global_device_ids=true, to_apply=%add | all-reduce | flops 512 | bytes 4096
  614.4 0.8 convolution_multiply_fusion
  (86 shorter events, 11.9 us)
Async XLA Ops:
  7.2 34.9 %copy-start = (bf16[1024,512]{1,0:T(8,128)(2,1)S(1)}, bf16[1024,512]{1,0:T(8,128)(2,1)}, u32[]{:S(2)}) copy-start(bf16[1024,512]{1,0:T(8,128)(2,1)} %param.15) | copy-start | bytes 3145732
  7.2 289.1 %all-reduce.4.cloned.1.call-start = ((), (), s32[]{:S(2)}) async-start(), calls=%async_computation.1 | async-start | bytes 2097152
  8.5 25.2 %copy-start.3 = (bf16[128,512]{1,0:T(8,128)(2,1)S(1)}, bf16[128,512]{1,0:T(8,128)(2,1)}, u32[]{:S(2)}) copy-start(bf16[128,512]{1,0:T(8,128)(2,1)} %param.16) | copy-start | bytes 393220
  11.9 23.6 %copy-start.1 = (bf16[256,1024]{1,0:T(8,128)(2,1)S(1)}, bf16[256,1024]{1,0:T(8,128)(2,1)}, u32[]{:S(2)}) copy-start(bf16[256,1024]{1,0:T(8,128)(2,1)} %param.11) | copy-start | bytes 1572868
  12.0 25.2 %collective-permute-start = (bf16[256,512]{0,1:T(8,128)(2,1)S(1)}, bf16[256,512]{0,1:T(8,128)(2,1)}, u32[]{:S(2)}, u32[]{:S(2)}) collective-permute-start(bf16[256,512]{0,1:T(8,128)(2,1)S(1)} %pad_maximum_fusion.1), channel_id=1, source_target_pairs={{0,4},{4,8},{8,12},{12,16},{16,20},{20,24},{24,28},{28,32},{32,36}... | collective-permute-start | bytes 786440 | tf_op jit(solution)/shard_map/ppermute | solution.py:19
  17.0 20.2 %collective-permute-start.1 = (bf16[256,512]{0,1:T(8,128)(2,1)S(1)}, bf16[256,512]{0,1:T(8,128)(2,1)}, u32[]{:S(2)}, u32[]{:S(2)}) collective-permute-start(bf16[256,512]{0,1:T(8,128)(2,1)S(1)} %pad_maximum_fusion.1), channel_id=1, source_target_pairs={{4,0},{8,4},{12,8},{16,12},{20,16},{24,20},{28,24},{32,28},{36,32}... | collective-permute-start | bytes 786440 | tf_op jit(solution)/shard_map/ppermute | solution.py:21
  19.2 16.5 %copy-start.5 = (f32[1024]{0:T(1024)S(1)}, f32[1024]{0:T(1024)}, u32[]{:S(2)}) copy-start(f32[1024]{0:T(1024)} %param.12) | copy-start | bytes 12292
  35.1 381.2 %all-gather.5.cloned.1.call-start = ((), (), s32[]{:S(2)}) async-start(), calls=%async_computation | async-start | bytes 1052672 | tf_op jit(solution)/shard_map/all_gather | solution.py:110
  40.1 1.6 copy-start.2
  40.1 4.1 copy-start.4
Sparse Core Ops, SparseCore 0:
  35.2 261.0 all-reduce.3
  300.6 103.6 all-gather.4
where the time goes:
time: 624 us; the launch traced here: 622 us
  blocking collectives  311 us (50%)
  waiting for transfers between devices  252 us (40%)
  between operations  15 us (2%)
  local copies, waits for them, and re-layouts  13.2 us (2%)
  matrix products  12.3 us (2%)
  other arithmetic  11 us (2%)
  starting transfers between devices  7.3 us (1%)
    unnamed x3, waiting for transfers between devices  252 us
    all_gather x1, blocking collectives, local(): lax.all_gather(caption_own, ('seq', 'head'), axis=0, tiled=True)  118 us
    all_gather x1, blocking collectives, local(): lax.all_gather(interval_embedding_rows, ('seq', 'head'), axis=0, tiled=True)  117 us
    unnamed x1, blocking collectives  75.9 us
  transfers between devices with their start and end apart: 4, of which 1 were waited for; matrix products, arithmetic and copies ran while one was open for 4% of the time, Pallas kernels for 0%

commit v1 on v0

v1 whole, which is shorter than its diff:
```python
import functools

import jax
import jax.numpy as jnp
from jax import lax
from jax.experimental import pallas as pl
from jax.experimental.pallas import tpu as pltpu
from jax.sharding import PartitionSpec as P

HDIM = 64
E = 512
BLK = 128
F = 256
D = 1024
HC = 256
LH = HC // HDIM
CAPS = 512
ZL = 16
NX, NY, NZ = 4, 4, 8
XY = NX * NY
MESH = pl.DeviceIdType.MESH
F32, BF16 = jnp.float32, jnp.bfloat16
NT = (((1,), (1,)), ((), ()))
NN = (((1,), (0,)), ((), ()))


def dot(a, b, dims=NN):
    return lax.dot_general(a, b, dims, preferred_element_type=F32)


def dot_split(a, b):
    hi = a.astype(BF16)
    lo = (a - hi.astype(F32)).astype(BF16)
    both = dot(jnp.concatenate([hi, lo], axis=0), b)
    n = a.shape[0]
    return both[:n] + both[n:]


def kernel(
    frames_h, gain_h, wqkv_h, wout_h, wproj_h, table_h, ids_h, bounds_s, div_s,
    grad_ref, loss_ref,
    frames, gain, wk, wv, wq, wout, wproj, tab, ids,
    k_own, vt_own, k_halo, vt_halo, acc_scr, ml_scr, att,
    rs_src, rs_buf, zb_src, zb_buf, caps,
    t1_src, t1_buf, t2_f, t2_src, t2_buf,
    spans, lt,
    ld, kv_s, kv_r, tab_sem, rs_s, rs_r, zb_s, zb_r, ag_s, ag_r, rl_s, rl_r,
    t1_s, t1_r, t2_s, t2_r,
):
    seq, head = lax.axis_index("seq"), lax.axis_index("head")
    core = lax.rem(seq, 2)
    zl = lax.rem(seq, ZL)
    xpos = lax.div(seq, ZL)
    zpos = lax.div(zl, 2)
    xy = xpos * NY + head
    slot = seq * NY + head
    partner = (seq + 1 - 2 * core, head)

    def z_dev(t):
        return (xpos * ZL + t, head)

    def xy_dev(t):
        return (lax.div(t, NY) * ZL + zl, lax.rem(t, NY))

    loads = [
        pltpu.make_async_copy(ids_h.at[:, pl.ds(core * 256, 256)], ids, ld.at[0]),
        pltpu.make_async_copy(frames_h, frames, ld.at[1]),
        pltpu.make_async_copy(gain_h, gain, ld.at[2]),
        pltpu.make_async_copy(wqkv_h.at[1], wk, ld.at[3]),
        pltpu.make_async_copy(wqkv_h.at[2], wv, ld.at[4]),
        pltpu.make_async_copy(wqkv_h.at[0], wq, ld.at[5]),
        pltpu.make_async_copy(table_h, tab.at[core], ld.at[6]),
        pltpu.make_async_copy(wout_h, wout, ld.at[7]),
        pltpu.make_async_copy(wproj_h, wproj, ld.at[8]),
    ]
    for c in loads:
        c.start()

    barrier = pltpu.get_barrier_semaphore()

    def greet(k, _):
        pl.semaphore_signal(
            barrier, inc=1, device_id=z_dev(lax.rem(zl + k, ZL)), device_id_type=MESH
        )
        pl.semaphore_signal(
            barrier, inc=1, device_id=xy_dev(lax.rem(xy + k, XY)), device_id_type=MESH
        )
        return 0

    lax.fori_loop(1, XY, greet, 0)
    line_end = jnp.logical_and(zl == ZL - 1, xpos < NX - 1)
    line_start = jnp.logical_and(zl == 0, xpos > 0)

    @pl.when(line_end)
    def _():
        pl.semaphore_signal(barrier, inc=1, device_id=(seq + 1, head), device_id_type=MESH)

    @pl.when(line_start)
    def _():
        pl.semaphore_signal(barrier, inc=1, device_id=(seq - 1, head), device_id_type=MESH)

    loads[0].wait()
    lane = lax.broadcasted_iota(jnp.int32, (256, 256), 1)
    first_slot = slot - core * NY
    vocab = (first_slot + NY * lax.div(lane, 128)) * 128 + lax.rem(lane, 128)
    tokens = ids[...].T
    counts = jnp.zeros((256, 256), F32)
    for t in range(16):
        counts = counts + jnp.where(tokens[:, t : t + 1] == vocab, 1.0, 0.0)
    counts = counts.astype(BF16)

    loads[1].wait()
    loads[2].wait()
    x32 = frames[...].astype(F32)
    scale = lax.rsqrt(jnp.sum(x32 * x32, axis=1, keepdims=True) * (1.0 / D) + 1e-5)
    normed = (x32 * scale * gain[...]).astype(BF16)
    loads[3].wait()
    k_own[...] = dot(normed, wk[...]).astype(BF16)
    loads[4].wait()
    vt_own[...] = dot(normed, wv[...]).T.astype(BF16)

    extra = line_end.astype(jnp.int32) + line_start.astype(jnp.int32)
    pl.semaphore_wait(barrier, 2 * (XY - 1) + extra)

    def halo(side, part):
        target = (seq + 1 - 2 * side, head)
        src, dst = ((k_own, k_halo), (vt_own, vt_halo))[part]
        return pltpu.make_async_remote_copy(
            src_ref=src, dst_ref=dst.at[side],
            send_sem=kv_s.at[2 * side + part], recv_sem=kv_r.at[2 * side + part],
            device_id=target, device_id_type=MESH,
        )

    last = NX * ZL - 1
    for part in (0, 1):
        @pl.when(seq < last)
        def _():
            halo(0, part).start()

        @pl.when(seq > 0)
        def _():
            halo(1, part).start()

    tab_copy = pltpu.make_async_remote_copy(
        src_ref=table_h, dst_ref=tab.at[core],
        send_sem=tab_sem.at[0], recv_sem=tab_sem.at[1],
        device_id=partner, device_id_type=MESH,
    )
    tab_copy.start()

    @pl.when(seq == 0)
    def _():
        k_halo[0] = jnp.zeros((F, HC), BF16)
        vt_halo[0] = jnp.zeros((HC, F), BF16)

    @pl.when(seq == last)
    def _():
        k_halo[1] = jnp.zeros((F, HC), BF16)
        vt_halo[1] = jnp.zeros((HC, F), BF16)

    loads[5].wait()
    q = (dot(normed, wq[...]).astype(BF16).astype(F32) * HDIM ** (-0.5)).astype(BF16)
    qm = [
        jnp.where(lax.div(lane, HDIM) == h, q.astype(F32), 0.0).astype(BF16) for h in range(LH)
    ]
    for h in range(LH):
        s = dot(k_own[...], qm[h], NT)
        m = jnp.max(s, axis=0, keepdims=True)
        p = jnp.exp(s - m)
        ml_scr[h, 0:1] = m
        ml_scr[h, 1:2] = jnp.sum(p, axis=0, keepdims=True)
        acc_scr[pl.ds(h * HDIM, HDIM), :] = dot(vt_own[pl.ds(h * HDIM, HDIM), :], p.astype(BF16))

    loads[6].wait()
    tab_copy.wait_recv()
    part_sums = dot(counts, tab[...].reshape(256, E))
    rs_src[...] = part_sums.astype(BF16).reshape(XY, 16, E)

    def rs_copy(target, here):
        return pltpu.make_async_remote_copy(
            src_ref=rs_src.at[target], dst_ref=rs_buf.at[here],
            send_sem=rs_s.at[target], recv_sem=rs_r.at[here],
            device_id=xy_dev(target), device_id_type=MESH,
        )

    def rs_start(k, _):
        rs_copy(lax.rem(xy + k, XY), xy).start()
        return 0

    lax.fori_loop(1, XY, rs_start, 0)
    rs_buf[pl.ds(xy, 1)] = rs_src[pl.ds(xy, 1)]

    @pl.when(seq > 0)
    def _():
        halo(0, 0).wait_recv()

    @pl.when(seq < last)
    def _():
        halo(1, 0).wait_recv()

    key_id = lax.broadcasted_iota(jnp.int32, (F, F), 0)
    left_ok = jnp.logical_and(key_id >= lane, seq > 0)
    right_ok = jnp.logical_and(key_id <= lane, seq < last)

    @pl.when(seq > 0)
    def _():
        halo(0, 1).wait_recv()

    @pl.when(seq < last)
    def _():
        halo(1, 1).wait_recv()

    for h in range(LH):
        rows = pl.ds(h * HDIM, HDIM)
        sl = jnp.where(left_ok, dot(k_halo[0], qm[h], NT), -1e30)
        sr = jnp.where(right_ok, dot(k_halo[1], qm[h], NT), -1e30)
        m0, l0 = ml_scr[h, 0:1], ml_scr[h, 1:2]
        m = jnp.maximum(m0, jnp.max(jnp.maximum(sl, sr), axis=0, keepdims=True))
        pleft, pright = jnp.exp(sl - m), jnp.exp(sr - m)
        alpha = jnp.exp(m0 - m)
        total = l0 * alpha + jnp.sum(pleft + pright, axis=0, keepdims=True)
        acc = (
            acc_scr[rows, :] * alpha
            + dot(vt_halo[0, rows, :], pleft.astype(BF16))
            + dot(vt_halo[1, rows, :], pright.astype(BF16))
        )
        att[rows, :] = (acc * (1.0 / total)).astype(BF16)

    row8 = lax.broadcasted_iota(jnp.int32, (8, F), 0)
    pick = jnp.where(lax.div(lax.broadcasted_iota(jnp.int32, (8, F), 1), BLK) == row8, 1.0, 0.0)
    pick = pick.astype(BF16)
    loads[7].wait()
    loads[8].wait()
    out_sums = dot(pick, att[...], NT)
    frame_sums = dot(pick, frames[...])
    own_cols = lax.div(lax.broadcasted_iota(jnp.int32, (8, D), 1), HC) == head
    through = dot_split(out_sums, wout[...]) + jnp.where(own_cols, frame_sums, 0.0)
    partial = dot_split(through, wproj[...])
    lane_e = lax.broadcasted_iota(jnp.int32, (8, E), 1)
    row_e = lax.broadcasted_iota(jnp.int32, (8, E), 0)
    for r in range(2):
        for side in range(2):
            edge = lax.div(bounds_s[r, side], BLK).astype(F32)
            partial = jnp.where(
                jnp.logical_and(row_e == 2 + side, lane_e == slot * 2 + r), edge, partial
            )
    t1_src[...] = partial[:4]

    def t1_copy(target, here):
        return pltpu.make_async_remote_copy(
            src_ref=t1_src, dst_ref=t1_buf.at[here],
            send_sem=t1_s.at[target], recv_sem=t1_r.at[here],
            device_id=xy_dev(target), device_id_type=MESH,
        )

    def t1_start(k, _):
        t1_copy(lax.rem(xy + k, XY), xy).start()
        return 0

    lax.fori_loop(1, XY, t1_start, 0)
    t1_buf[pl.ds(xy, 1)] = partial[:4].reshape(1, 4, E)

    def rs_wait(k, _):
        rs_copy(xy, lax.rem(xy + k, XY)).wait_recv()
        return 0

    lax.fori_loop(1, XY, rs_wait, 0)
    zb_src[...] = jnp.sum(rs_buf[...].astype(F32), axis=0).astype(BF16)

    def zb_copy(target, here):
        return pltpu.make_async_remote_copy(
            src_ref=zb_src, dst_ref=zb_buf.at[here],
            send_sem=zb_s.at[target], recv_sem=zb_r.at[here],
            device_id=z_dev(target * 2 + core), device_id_type=MESH,
        )

    def zb_start(k, _):
        zb_copy(lax.rem(zpos + k, NZ), zpos).start()
        return 0

    lax.fori_loop(1, NZ, zb_start, 0)
    zb_buf[pl.ds(zpos, 1)] = zb_src[...].reshape(1, 16, E)

    def t1_wait(k, _):
        t1_copy(xy, lax.rem(xy + k, XY)).wait_recv()
        return 0

    lax.fori_loop(1, XY, t1_wait, 0)
    t2_f[...] = jnp.zeros((16, E), F32)
    edges = jnp.zeros((4, E), F32)
    for xx in range(NX):
        tot = jnp.sum(t1_buf[pl.ds(xx * NY, NY)], axis=0)
        t2_f[pl.ds(2 * xx, 2), :] = tot[0:2]
        edges = edges + tot
    t2_f[pl.ds(8, 2), :] = edges[2:4]
    t2_src[...] = t2_f[...].astype(BF16)

    def t2_copy(target, here):
        return pltpu.make_async_remote_copy(
            src_ref=t2_src, dst_ref=t2_buf.at[here],
            send_sem=t2_s.at[target], recv_sem=t2_r.at[here],
            device_id=z_dev(target), device_id_type=MESH,
        )

    def t2_start(k, _):
        t2_copy(lax.rem(zl + k, ZL), zl).start()
        return 0

    lax.fori_loop(1, ZL, t2_start, 0)
    t2_buf[pl.ds(zl, 1)] = t2_f[...].astype(BF16).reshape(1, 16, E)

    def zb_wait(k, _):
        zb_copy(zpos, lax.rem(zpos + k, NZ)).wait_recv()
        return 0

    lax.fori_loop(1, NZ, zb_wait, 0)

    def unit_rows(v):
        mean = jnp.sum(v * v, axis=1, keepdims=True) * (1.0 / E)
        return v * lax.rsqrt(mean + 1e-6) * E ** (-0.5)

    own = unit_rows(jnp.sum(zb_buf[...].astype(F32), axis=0)).astype(BF16)
    caps[pl.ds(core * XY + xy, 1)] = own.reshape(1, 16, E)

    def ag_copy(target, here):
        piece = caps.at[core * XY + here]
        return pltpu.make_async_remote_copy(
            src_ref=piece, dst_ref=piece, send_sem=ag_s.at[target], recv_sem=ag_r.at[here],
            device_id=xy_dev(target), device_id_type=MESH,
        )

    def rl_copy(here, side):
        piece = caps.at[side * XY + here]
        return pltpu.make_async_remote_copy(
            src_ref=piece, dst_ref=piece, send_sem=rl_s.at[here], recv_sem=rl_r.at[here],
            device_id=partner, device_id_type=MESH,
        )

    def ag_start(k, _):
        ag_copy(lax.rem(xy + k, XY), xy).start()
        return 0

    lax.fori_loop(1, XY, ag_start, 0)
    rl_copy(xy, core).start()

    def t2_wait(k, _):
        t2_copy(zl, lax.rem(zl + k, ZL)).wait_recv()
        return 0

    lax.fori_loop(1, ZL, t2_wait, 0)
    t2_all = t2_buf[...]
    edges = jnp.sum(t2_all.astype(F32), axis=0)[8:16]
    edges_t = edges.T
    col = lax.broadcasted_iota(jnp.int32, (BLK, 256), 1)
    sub = lax.rem(col, 16)
    block = lax.div(sub, 2) * (2 * ZL) + lax.div(col, 16) * 2 + lax.rem(sub, 2)
    block = jnp.where(sub < 8, block, -1).astype(F32)
    t2_flat = t2_all.reshape(256, E)
    for b in range(4):
        lower = edges_t[b * BLK : (b + 1) * BLK, 0:1]
        upper = edges_t[b * BLK : (b + 1) * BLK, 1:2]
        mask = jnp.where(
            jnp.logical_and(block >= lower, jnp.logical_and(block < upper, block >= 0.0)), 1.0, 0.0
        ).astype(BF16)
        spans[pl.ds(b * BLK, BLK), :] = unit_rows(dot(mask, t2_flat)).astype(BF16)

    def ag_wait(k, _):
        s = lax.rem(xy + k, XY)
        ag_copy(xy, s).wait_recv()
        rl_copy(s, core).start()
        return 0

    lax.fori_loop(1, XY, ag_wait, 0)

    def rl_wait(k, _):
        rl_copy(k, 1 - core).wait_recv()
        return 0

    lax.fori_loop(0, XY, rl_wait, 0)

    divisor = div_s[0]
    all_caps = caps[...].reshape(CAPS, E)
    row_sum = jnp.zeros((1, CAPS), F32)
    for b in range(4):
        part = dot(spans[pl.ds(b * BLK, BLK), :], all_caps, NT) * divisor
        lt[pl.ds(b * BLK, BLK), :] = part
        row_sum = row_sum + jnp.sum(jnp.exp(part), axis=0, keepdims=True)
    mine = lt[pl.ds(pl.multiple_of(seq * 8, 8), 8), :]
    expd = jnp.exp(mine)
    col_sum = jnp.sum(expd, axis=1, keepdims=True)
    is_diag = lane_e == row_e + seq * 8
    weights = (
        0.5 * expd * (1.0 / row_sum)
        + 0.5 * expd * (1.0 / col_sum)
        - jnp.where(is_diag, 1.0, 0.0)
    ).astype(BF16)
    grads = dot(weights, all_caps) * divisor
    losses = jnp.where(is_diag, 0.5 * (jnp.log(row_sum) + jnp.log(col_sum)) - mine, 0.0)
    out_lane = lax.broadcasted_iota(jnp.int32, (1, 128), 1)
    loss_row = jnp.zeros((1, 128), F32)
    for r in range(2):
        chosen = row_e == 2 * head + r
        grad_ref[r : r + 1, :] = jnp.sum(jnp.where(chosen, grads, 0.0), axis=0, keepdims=True)
        here = jnp.where(chosen, losses, 0.0)
        value = jnp.sum(jnp.sum(here, axis=0, keepdims=True), axis=1, keepdims=True)
        loss_row = jnp.where(out_lane == r, value, loss_row)
    loss_ref[...] = loss_row

    for part in (0, 1):
        @pl.when(seq < last)
        def _():
            halo(0, part).wait_send()

        @pl.when(seq > 0)
        def _():
            halo(1, part).wait_send()

    tab_copy.wait_send()

    def drain_xy(k, _):
        t = lax.rem(xy + k, XY)
        rs_copy(t, xy).wait_send()
        t1_copy(t, xy).wait_send()
        ag_copy(t, xy).wait_send()
        t2_copy(lax.rem(zl + k, ZL), zl).wait_send()
        rl_copy(t, core).wait_send()
        return 0

    lax.fori_loop(1, XY, drain_xy, 0)
    rl_copy(xy, core).wait_send()

    def drain_z(k, _):
        zb_copy(lax.rem(zpos + k, NZ), zpos).wait_send()
        return 0

    lax.fori_loop(1, NZ, drain_z, 0)


def local(
    frames, norm_gain, w_qkv, w_out, w_proj, text_table, token_ids, span_bounds, contrast_divisor
):
    any_spec = pl.BlockSpec(memory_space=pltpu.HBM)
    smem = pl.BlockSpec(memory_space=pltpu.SMEM)
    vmem = pl.BlockSpec(memory_space=pltpu.VMEM)
    dma = pltpu.SemaphoreType.DMA
    grad, loss = pl.pallas_call(
        kernel,
        out_shape=(
            jax.ShapeDtypeStruct((2, E), F32),
            jax.ShapeDtypeStruct((1, 128), F32),
        ),
        in_specs=[any_spec] * 7 + [smem] * 2,
        out_specs=(vmem, vmem),
        scratch_shapes=[
            pltpu.VMEM((F, D), BF16),
            pltpu.VMEM((1, D), F32),
            pltpu.VMEM((D, HC), BF16),
            pltpu.VMEM((D, HC), BF16),
            pltpu.VMEM((D, HC), BF16),
            pltpu.VMEM((HC, D), BF16),
            pltpu.VMEM((D, E), BF16),
            pltpu.VMEM((2, 128, E), BF16),
            pltpu.VMEM((16, 256), jnp.int32),
            pltpu.VMEM((F, HC), BF16),
            pltpu.VMEM((HC, F), BF16),
            pltpu.VMEM((2, F, HC), BF16),
            pltpu.VMEM((2, HC, F), BF16),
            pltpu.VMEM((HC, F), F32),
            pltpu.VMEM((LH, 8, F), F32),
            pltpu.VMEM((HC, F), BF16),
            pltpu.VMEM((XY, 16, E), BF16),
            pltpu.VMEM((XY, 16, E), BF16),
            pltpu.VMEM((16, E), BF16),
            pltpu.VMEM((NZ, 16, E), BF16),
            pltpu.VMEM((2 * XY, 16, E), BF16),
            pltpu.VMEM((4, E), F32),
            pltpu.VMEM((XY, 4, E), F32),
            pltpu.VMEM((16, E), F32),
            pltpu.VMEM((16, E), BF16),
            pltpu.VMEM((ZL, 16, E), BF16),
            pltpu.VMEM((CAPS, E), BF16),
            pltpu.VMEM((CAPS, CAPS), F32),
            dma((9,)),
            dma((4,)), dma((4,)),
            dma((2,)),
            dma((XY,)), dma((XY,)),
            dma((NZ,)), dma((NZ,)),
            dma((XY,)), dma((XY,)),
            dma((XY,)), dma((XY,)),
            dma((XY,)), dma((XY,)),
            dma((ZL,)), dma((ZL,)),
        ],
        compiler_params=pltpu.CompilerParams(
            collective_id=0, has_side_effects=True, vmem_limit_bytes=67043328
        ),
        name="spans",
    )(
        frames, norm_gain.reshape(1, D), w_qkv, w_out, w_proj, text_table, token_ids.T,
        span_bounds, contrast_divisor,
    )
    return grad, loss[0, :2]


def solution(mesh):
    placed = (
        P("seq", None),
        P(),
        P(None, None, "head"),
        P("head", None),
        P(),
        P(("seq", "head"), None),
        P(),
        P(("seq", "head"), None),
        P(),
    )
    return jax.shard_map(
        local,
        mesh=mesh,
        in_specs=placed,
        out_specs=(P(("seq", "head"), None), P(("seq", "head"))),
        check_vma=False,
    )
```

time: 624 us -> 41.3 us (0.07)
  blocking collectives: 311 us -> 0 us
  waiting for transfers between devices: 252 us -> 0 us
  Pallas kernels: 0 us -> 37.5 us
  between operations: 15 us -> 1.29 us
  matrix products: 12.3 us -> 0 us
  other arithmetic: 11 us -> 0 us
  local copies, waits for them, and re-layouts: 13.2 us -> 2.4 us
  starting transfers between devices: 7.3 us -> 0 us
    unnamed x3 -> x0, waiting for transfers between devices: 252 us -> none
    all_gather x2 -> x0, blocking collectives: 235 us -> none  [the longest x1 118 us: local(): lax.all_gather(caption_own, ('seq', 'head'), axis=0, tiled=True)]
    unnamed x1 -> x0, blocking collectives: 75.9 us -> none
    pallas_call x0 -> x1, Pallas kernels: none -> 37.5 us  [local(): pl.pallas_call(kernel, out_shape=(jax.ShapeDtypeStruct((2, E), F32), jax....]
    dot_general x13 -> x0, matrix products: 12.3 us -> none  [the longest x1 1.7 us: local(): jnp.dot(normed, w_qkv[2], preferred_element_type=jnp.float32)]
    dynamic_slice x17 -> x0, local copies, waits for them, and re-layouts: 11.7 us -> none  [the longest x16 11.6 us: add_token(): column = lax.dynamic_index_in_dim(chosen, position, 1, keepdims=False)]
    ppermute x2 -> x0, starting transfers between devices: 7.22 us -> none  [the longest x1 5.06 us: extended(): lax.ppermute(tail, axis, [(i, (i + 1) % count) for i in range(ends)])]
  transfers between devices with their start and end apart: 4 -> 0, of which waited for: 1 -> 0; matrix products, arithmetic and copies ran while one was open for 4% -> 0% of each run, Pallas kernels for 0% -> 0%
where the time goes in v1:
time: 41.3 us; the launch traced here: 41.2 us
  Pallas kernels  37.5 us (91%)
  local copies, waits for them, and re-layouts  2.4 us (6%)
  between operations  1.29 us (3%)
    pallas_call x1, Pallas kernels, local(): pl.pallas_call(kernel, out_shape=(jax.ShapeDtypeStruct((2, E), F32), jax....  37.5 us
    unnamed x1, local copies, waits for them, and re-layouts  1.26 us
    squeeze x1, local copies, waits for them, and re-layouts, local(): return (grad, loss[0, :2])  1.14 us

profile of v1, /device:TPU:1, one launch (start us, length us, event | category | flops | bytes accessed | tf_op | source)
XLA Modules:
  0.0 41.2 jit_solution(1909317191476814021)
XLA Ops:
  1.3 37.5 %spans.1 = (f32[2,512]{1,0:T(2,128)}, f32[1,128]{1,0:T(1,128)}) custom-call(bf16[256,1024]{1,0:T(8,128)(2,1)} %frames_h.1, f32[1,1024]{1,0:T(1,128)} %bitcast.5, bf16[3,1024,256]{2,1,0:T(8,128)(2,1)} %wqkv_h.1, bf16[256,1024]{1,0:T(8,128)(2,1)} %wout_h.1, bf16[1024,512]{1,0:T(8,128)(2,1)} %wproj_h.1, bf16[128,512]{1,0:T(8,128)(2,1)} %table_h.1, ...), custom_call_target="tpu_custom_call" | custom-call | tf_op jit(solution)/shard_map/spans/pallas_call | solution.py:446
  38.8 1.1 %slice_bitcast_fusion = f32[2]{0:T(128)} fusion(f32[1,128]{1,0:T(1,128)} %get-tuple-element.5), kind=kLoop, calls=%fused_computation | loop fusion | bytes 16 | tf_op jit(solution)/shard_map/squeeze | solution.py:501
  39.9 1.3 %copy.13 = f32[2,512]{1,0:T(2,128)} copy(f32[2,512]{1,0:T(2,128)} %get-tuple-element.8) | data formatting | bytes 8192
